TPU v7x, 32 devices: a whole 2x2x4 slice. The times are simulated.
32 devices in a mesh: group: 2 (over y), tm: 4 (over z), seq: 2 (over x), mp: 2 (over core).
Axes of the slice: x: 2, y: 2, z: 4, core: 2. Of those that a mesh axis runs over, the one named last changes fastest.
Arguments:
- states: bfloat16 [8, 128, 5120], P(('group', 'tm'), 'seq'), parts along dimension 0, may hold values from -6 to 6
- start_step: int32 [2], P('group'), parts along dimension 0, may hold values from 0 to 96
- w_qkv: bfloat16 [3, 5120, 3072], P(None, 'tm', ('seq', 'mp')), may hold values from -0.078125 to 0.078125
- qk_gain: float32 [2, 3072], P(None, ('seq', 'mp')), may hold values from 0.25 to 1.75
- w_out: bfloat16 [5120, 3072], P('tm', ('seq', 'mp')), may hold values from -0.109375 to 0.109375
- time_proj: bfloat16 [256, 15360], P('tm'), may hold values from -0.375 to 0.375
Outputs:
- displacement: float32 [8, 128, 5120], P(('group', 'tm'), 'seq', 'mp'), parts along dimension 0
There are 2 independent parts, one for each index of `group`. A program takes and returns all parts, laid end to end along the dimension named above; an argument that names none is the same for every part. Nothing has to cross between parts.
Inputs may be any that keep to these rules, and one draw needn't show every extreme that they name: `start_step`: the window lies inside the trajectory.
All inputs are finite; a program needn't handle non-finite values.
Results may differ from a plain program's by a relative error of at most 0.0029.
Values may be sent and summed in bfloat16 or wider, within the bound.
No kernel may reach another device: no remote copies, remote signals or barrier semaphores. Data moves between devices by JAX's collectives and lax.ppermute only.
A program may use at most 128 MiB of HBM per device.

v0:
```python
import jax
import jax.numpy as jnp
from jax import lax
from jax.sharding import PartitionSpec as P

HEAD_DIM = 128
FREQ = 256
STEPS = 100
sample_shift = 5.0
norm_eps = 1e-06


def from_behind(block, axis, distance):
    devices = range(lax.axis_size(axis))
    route = [(i - distance, i) for i in devices if i - distance in devices]
    return lax.ppermute(block, axis, route)


def sigma_of(index):
    unit = 1.0 - index.astype(jnp.float32) / jnp.float32(STEPS)
    return sample_shift * unit / (1.0 + (sample_shift - 1.0) * unit)


def embed_time(sigma_now):
    half_freq = FREQ // 2
    ranks = jnp.arange(half_freq).astype(jnp.float32)
    freqs = jnp.exp(-jnp.log(jnp.float32(10000.0)) * ranks / jnp.float32(half_freq))
    angles = (1000.0 * sigma_now)[:, None] * freqs[None, :]
    return jnp.concatenate([jnp.cos(angles), jnp.sin(angles)], axis=1).astype(jnp.bfloat16)


def head_norm(values, gain, frames, seq_len, heads_dev):
    shaped = values.reshape(frames, seq_len, heads_dev, HEAD_DIM)
    meansq = jnp.mean(shaped * shaped, axis=-1, keepdims=True)
    scaled = shaped * lax.rsqrt(meansq + norm_eps) * gain.reshape(heads_dev, HEAD_DIM)
    return scaled.astype(jnp.bfloat16)


def attend(query, keys, values):
    frames, seq_len, heads_dev, head_size = query.shape
    block = min(seq_len, 512)
    blocks = seq_len // block
    inv_root = 1.0 / jnp.sqrt(jnp.float32(head_size))
    stacked = query.reshape(frames, blocks, block, heads_dev, head_size).transpose(1, 0, 2, 3, 4)

    def one_block(q_block):
        scores = (
            jnp.einsum("wqhd,wkhd->whqk", q_block, keys, preferred_element_type=jnp.float32)
            * inv_root
        )
        expo = jnp.exp(scores)
        probs = (expo / jnp.sum(expo, axis=-1, keepdims=True)).astype(jnp.bfloat16)
        return jnp.einsum(
            "whqk,wkhd->wqhd", probs, values, preferred_element_type=jnp.float32
        ).astype(jnp.bfloat16)

    result = lax.map(one_block, stacked)
    return result.transpose(1, 0, 2, 3, 4).reshape(frames, seq_len, heads_dev * head_size)


def on_device(states, start_step, w_qkv, qk_gain, w_out, time_proj):
    frames, tok, width = states.shape
    n_tm = lax.axis_size("tm")
    n_mp = lax.axis_size("mp")
    window = frames * n_tm
    tm_pos = lax.axis_index("tm")
    steps_idx = start_step[0] + jnp.arange(window)
    sigma_now = sigma_of(steps_idx)
    step_size = sigma_of(steps_idx + 1) - sigma_now
    emb = embed_time(sigma_now)
    freq_rows = time_proj.shape[0]
    emb_cols = lax.dynamic_slice_in_dim(emb, tm_pos * freq_rows, freq_rows, 1)
    modulation = lax.psum_scatter(
        jnp.dot(emb_cols, time_proj, preferred_element_type=jnp.float32),
        "tm",
        scatter_dimension=0,
        tiled=True,
    )
    shift = modulation[:, :width]
    scale = modulation[:, width : 2 * width]
    gate = modulation[:, 2 * width :]
    field = states.astype(jnp.float32)
    mean = jnp.mean(field, axis=-1, keepdims=True)
    centred = field - mean
    var = jnp.mean(centred * centred, axis=-1, keepdims=True)
    normed = centred * lax.rsqrt(var + norm_eps)
    hidden = (normed * (1.0 + scale[:, None, :]) + shift[:, None, :]).astype(jnp.bfloat16)
    whole = lax.all_gather(hidden, "seq", axis=1, tiled=True)
    seq_len = whole.shape[1]
    flat = whole.reshape(frames * seq_len, width)
    head_cols = w_qkv.shape[2]
    heads_dev = head_cols // HEAD_DIM
    proj = jnp.einsum(
        "rd,cdh->crh",
        flat,
        lax.all_gather(w_qkv, "tm", axis=1, tiled=True),
        preferred_element_type=jnp.float32,
    )
    query = head_norm(proj[0], qk_gain[0], frames, seq_len, heads_dev)
    keys = head_norm(proj[1], qk_gain[1], frames, seq_len, heads_dev)
    values = proj[2].astype(jnp.bfloat16).reshape(frames, seq_len, heads_dev, HEAD_DIM)
    attn = attend(query, keys, values)
    out_full = lax.all_gather(w_out, "tm", axis=0, tiled=True)
    half_width = width // n_mp
    rows = frames * tok
    first = jnp.int32(0) // rows
    pieces = []
    for offset in range(rows * lax.axis_size(("seq", "mp")) // rows):
        owner = first + offset
        segment = owner // n_mp
        column = owner % n_mp
        tokens_part = lax.dynamic_slice_in_dim(attn, segment * tok, tok, 1)
        weight_part = lax.dynamic_slice_in_dim(out_full, column * half_width, half_width, 0)
        product = jnp.einsum(
            "tsh,eh->tse", tokens_part, weight_part, preferred_element_type=jnp.float32
        )
        pieces.append(product.reshape(rows, half_width))
    out_part = lax.psum_scatter(
        jnp.concatenate(pieces, axis=0), ("seq", "mp"), scatter_dimension=0, tiled=True
    ).reshape(frames, tok, half_width)
    gate_own = lax.dynamic_slice_in_dim(gate, lax.axis_index("mp") * half_width, half_width, 1)
    own_steps = lax.dynamic_slice_in_dim(step_size, tm_pos * frames, frames, 0)
    drift = gate_own[:, None, :] * out_part
    increments = own_steps[:, None, None] * drift
    local_sums = jnp.cumsum(increments, axis=0)
    block_total = local_sums[-1]
    running = block_total
    for level in range((n_tm - 1).bit_length()):
        running = running + from_behind(running, "tm", 1 << level)
    before = running - block_total
    return before[None, :, :] + local_sums


def solution(mesh):
    return jax.shard_map(
        on_device,
        mesh=mesh,
        in_specs=(
            P(("group", "tm"), "seq", None),
            P("group"),
            P(None, "tm", ("seq", "mp")),
            P(None, ("seq", "mp")),
            P("tm", ("seq", "mp")),
            P("tm", None),
        ),
        out_specs=P(("group", "tm"), "seq", "mp"),
        check_vma=False,
    )
```

profile of v0, /device:TPU:25, one launch (start us, length us, event | category | flops | bytes accessed | tf_op | source)
XLA Modules:
  0.0 721.7 jit_solution(13477119722304982495)
XLA Ops:
  6.5 0.0 copy-start
  6.5 0.0 copy-start.6
  6.5 0.0 copy-start.2
  6.5 0.0 all-reduce.3.cloned.1.call-start
  7.4 0.5 divide_subtract_fusion
  7.9 0.1 fusion.24
  8.0 0.3 copy-done
  8.3 1.1 fusion.26
  9.4 0.0 all-reduce.3.cloned.1.call-update
  9.5 0.0 all-gather.4.cloned.1.call-start
  9.5 0.0 copy-done.2
  9.5 0.2 convert_reduce_fusion
  9.7 0.3 fusion.10
  10.1 0.0 copy-done.6
  10.1 0.6 dynamic-slice.1
  10.7 32.4 %all-reduce.3.cloned.1.call-done = f32[4,15360]{1,0:T(4,128)} async-done(((f32[4,15360]{1,0:T(4,128)}), f32[4,15360]{1,0:T(4,128)}) %all-reduce.3.cloned.1.call-update) | async-done | bytes 245776
  43.0 1.7 dynamic-slice_add_fusion
  44.7 1.1 fusion.13
  45.8 0.0 all-gather.4.cloned.1.call-update
  45.9 0.0 copy-start.4
  45.9 0.0 all-gather.6.cloned.1.call-start
  45.9 0.7 all-gather.6.cloned.1.call-update
  46.6 0.0 all-gather.8.cloned.1.call-start
  46.7 0.5 all-gather.8.cloned.1.call-update
  47.2 0.0 reduce-scatter.2.cloned.1.call-start
  47.2 0.0 copy-done.4
  47.3 25.9 %all-gather.4.cloned.1.call-done = bf16[1,128,5120]{2,1,0:T(8,128)(2,1)} async-done(((bf16[1,64,5120]{2,1,0:T(8,128)(2,1)}), bf16[1,128,5120]{2,1,0:T(8,128)(2,1)}) %all-gather.4.cloned.1.call-update) | async-done | bytes 1310736 | tf_op jit(solution)/shard_map/all_gather | solution.py:88
  73.2 398.3 %all-gather.6.cloned.1.call-done = bf16[3,5120,768]{2,1,0:T(8,128)(2,1)} async-done(((bf16[3,1280,768]{2,1,0:T(8,128)(2,1)}), bf16[3,5120,768]{2,1,0:T(8,128)(2,1)}) %all-gather.6.cloned.1.call-update) | async-done | bytes 23592976 | tf_op jit(solution)/shard_map/all_gather | solution.py:96
  471.4 10.0 %convolution_bitcast_fusion = f32[3,128,768]{2,1,0:T(8,128)S(1)} fusion(bf16[3,5120,768]{2,1,0:T(8,128)(2,1)} %all-gather.6.cloned.1.call-done, bf16[1,128,5120]{2,1,0:T(8,128)(2,1)} %all-gather.4.cloned.1.call-done), kind=kOutput, calls=%fused_computation.13 | convolution fusion | flops 3019898880 | bytes 26083328 | tf_op jit(solution)/shard_map/rd,cdh->crh/dot_general | solution.py:93
  481.4 0.7 slice.45
  482.1 0.1 slice_multiply_fusion.1
  482.3 0.9 copy.23
  483.2 0.2 copy.21
  483.3 1.1 reduce_sum.49
  484.5 0.2 copy.22
  484.6 0.2 copy.20
  484.8 1.1 copy.19
  485.9 0.5 fusion.15
  486.4 0.2 convolution_convert_fusion
  486.7 125.4 %all-gather.8.cloned.1.call-done = bf16[5120,768]{1,0:T(8,128)(2,1)} async-done(((bf16[1280,768]{1,0:T(8,128)(2,1)}), bf16[5120,768]{1,0:T(8,128)(2,1)}) %all-gather.8.cloned.1.call-update) | async-done | bytes 7864336 | tf_op jit(solution)/shard_map/all_gather | solution.py:103
  612.1 0.0 copy-start.1
  612.1 3.6 fusion.2
  615.7 3.6 fusion.4
  619.3 0.0 copy-done.1
  619.3 1.3 fusion.6
  620.6 1.5 fusion
  622.1 1.7 pad_maximum_fusion
  623.8 0.0 copy-start.5
  623.8 0.0 reduce-scatter.2.cloned.1.call-update
  623.8 0.6 copy-done.5
  624.3 0.6 dynamic_slice.28
  624.9 1.5 dynamic-slice_reduce_fusion
  626.4 32.9 %reduce-scatter.2.cloned.1.call-done = f32[64,2560]{1,0:T(8,128)} async-done(((f32[256,2560]{1,0:T(8,128)}), f32[64,2560]{1,0:T(8,128)}) %reduce-scatter.2.cloned.1.call-update) | async-done | bytes 655376 | tf_op jit(solution)/shard_map/reduce_scatter | solution.py:118
  659.4 0.0 copy-start.3
  659.4 1.8 multiply_multiply_fusion
  661.1 1.3 collective-permute-start
  662.4 16.1 %collective-permute-done = f32[64,2560]{1,0:T(8,128)S(1)} collective-permute-done((f32[64,2560]{1,0:T(8,128)S(1)}, f32[64,2560]{1,0:T(8,128)S(1)}, u32[]{:S(2)}, u32[]{:S(2)}) %collective-permute-start) | collective-permute-done | bytes 655392 | tf_op jit(solution)/shard_map/ppermute | solution.py:16
  678.5 1.7 fusion.35
  680.2 1.3 collective-permute-start.1
  681.5 32.1 %collective-permute-done.1 = f32[64,2560]{1,0:T(8,128)S(1)} collective-permute-done((f32[64,2560]{1,0:T(8,128)S(1)}, f32[64,2560]{1,0:T(8,128)S(1)}, u32[]{:S(2)}, u32[]{:S(2)}) %collective-permute-start.1) | collective-permute-done | bytes 655392 | tf_op jit(solution)/shard_map/ppermute | solution.py:16
  713.7 0.0 copy-done.3
  713.7 1.5 fusion.16
  (7 shorter events, 0.1 us)
Async XLA Ops:
  6.5 1.8 copy-start
  6.5 3.5 copy-start.6
  6.5 3.0 copy-start.2
  6.5 36.5 %all-reduce.3.cloned.1.call-start = ((), (), s32[]{:S(2)}) async-start(), calls=%async_computation.5 | async-start | bytes 491520
  9.5 63.7 %all-gather.4.cloned.1.call-start = ((), (), s32[]{:S(2)}) async-start(), calls=%async_computation.1 | async-start | bytes 1966080 | tf_op jit(solution)/shard_map/all_gather | solution.py:88
  45.9 1.4 copy-start.4
  45.9 425.6 %all-gather.6.cloned.1.call-start = ((), (), s32[]{:S(2)}) async-start(), calls=%async_computation.2 | async-start | bytes 29491200 | tf_op jit(solution)/shard_map/all_gather | solution.py:96
  46.6 565.5 %all-gather.8.cloned.1.call-start = ((), (), s32[]{:S(2)}) async-start(), calls=%async_computation.3 | async-start | bytes 9830400 | tf_op jit(solution)/shard_map/all_gather | solution.py:103
  47.2 612.2 %reduce-scatter.2.cloned.1.call-start = ((), (), s32[]{:S(2)}) async-start(), calls=%async_computation.4 | async-start | bytes 3276800 | tf_op jit(solution)/shard_map/reduce_scatter | solution.py:118
  612.1 7.1 copy-start.1
  623.8 0.6 copy-start.5
  659.4 54.3 %copy-start.3 = (f32[64,2560]{1,0:T(8,128)S(1)}, f32[64,2560]{1,0:T(8,128)}, u32[]{:S(2)}) copy-start(f32[64,2560]{1,0:T(8,128)} %reduce-scatter.2.cloned.1.call-done) | copy-start | bytes 1966084
  661.1 17.4 %collective-permute-start = (f32[64,2560]{1,0:T(8,128)S(1)}, f32[64,2560]{1,0:T(8,128)S(1)}, u32[]{:S(2)}, u32[]{:S(2)}) collective-permute-start(f32[64,2560]{1,0:T(8,128)S(1)} %multiply_multiply_fusion), channel_id=1, source_target_pairs={{0,4},{4,8},{8,12},{1,5},{5,9},{9,13},{2,6},{6,10},{10,14},{3,7},{... | collective-permute-start | bytes 1966088 | tf_op jit(solution)/shard_map/ppermute | solution.py:16
  680.2 33.4 %collective-permute-start.1 = (f32[64,2560]{1,0:T(8,128)S(1)}, f32[64,2560]{1,0:T(8,128)S(1)}, u32[]{:S(2)}, u32[]{:S(2)}) collective-permute-start(f32[64,2560]{1,0:T(8,128)S(1)} %fusion.35), channel_id=1, source_target_pairs={{0,8},{4,12},{1,9},{5,13},{2,10},{6,14},{3,11},{7,15},{16,24},{20,... | collective-permute-start | bytes 1966088 | tf_op jit(solution)/shard_map/ppermute | solution.py:16
Sparse Core Ops, SparseCore 0:
  9.7 33.3 all-reduce.2
  46.0 27.1 all-gather.3
  74.7 396.6 all-gather.5
  472.9 139.2 all-gather.7
  623.9 35.4 reduce-scatter.1
where the time goes:
time: 722 us
  waiting for transfers between devices  664 us (92%)
  matrix products  21.8 us (3%)
  between operations  14.1 us (2%)
  other arithmetic  12 us (2%)
    all_gather x1, waiting for transfers between devices, on_device(): lax.all_gather(w_qkv, 'tm', axis=1, tiled=True)  398 us
    all_gather x1, waiting for transfers between devices, on_device(): out_full = lax.all_gather(w_out, 'tm', axis=0, tiled=True)  125 us
    ppermute x2, waiting for transfers between devices, from_behind(): return lax.ppermute(block, axis, route)  48.2 us
    unnamed x6, waiting for transfers between devices  33.6 us
    reduce_scatter x1, waiting for transfers between devices, on_device(): lax.psum_scatter(jnp.concatenate(pieces, axis=0), ('seq', 'mp'), scatter_...  32.9 us
    all_gather x1, waiting for transfers between devices, on_device(): whole = lax.all_gather(hidden, 'seq', axis=1, tiled=True)  25.9 us
  transfers between devices with their start and end apart: 7, of which 7 were waited for; matrix products, arithmetic and copies ran while one was open for 3% of the time, Pallas kernels for 0%

commit v1 on v0

--- a/solution.py
+++ b/solution.py
@@ -100,7 +100,12 @@
     keys = head_norm(proj[1], qk_gain[1], frames, seq_len, heads_dev)
     values = proj[2].astype(jnp.bfloat16).reshape(frames, seq_len, heads_dev, HEAD_DIM)
     attn = attend(query, keys, values)
-    out_full = lax.all_gather(w_out, "tm", axis=0, tiled=True)
+    ring = [w_out]
+    for hop in range(3):
+        ring.append(lax.ppermute(ring[-1], "tm", [(dev, (dev + 1) % 4) for dev in range(4)]))
+    out_full = jnp.roll(
+        jnp.concatenate(ring[::-1], axis=0), (lax.axis_index("tm") + 1) * ring[0].shape[0], axis=0
+    )
     half_width = width // n_mp
     rows = frames * tok
     first = jnp.int32(0) // rows

time: 722 us -> 683 us (0.946)
  waiting for transfers between devices: 664 us -> 598 us
  local copies, waits for them, and re-layouts: 6.76 us -> 23.6 us
    ppermute x0 -> x3, waiting for transfers between devices: none -> 296 us  [on_device(): lax.ppermute(ring[-1], 'tm', [(dev, (dev + 1) % 4) for dev in range(4)])]
    all_gather x1, waiting for transfers between devices: 398 us -> 190 us  [on_device(): lax.all_gather(w_qkv, 'tm', axis=1, tiled=True)]
    all_gather x1 -> x0, waiting for transfers between devices: 125 us -> none  [on_device(): out_full = lax.all_gather(w_out, 'tm', axis=0, tiled=True)]
    all_gather x1, waiting for transfers between devices: 25.9 us -> 0.01 us  [on_device(): whole = lax.all_gather(hidden, 'seq', axis=1, tiled=True)]
    unnamed x15 -> x22, local copies, waits for them, and re-layouts: 1.47 us -> 19.3 us
    unnamed x6 -> x5, waiting for transfers between devices: 33.6 us -> 30.5 us
  transfers between devices with their start and end apart: 7 -> 9, of which waited for: 7 -> 8; matrix products, arithmetic and copies ran while one was open for 3% -> 3% of each run, Pallas kernels for 0% -> 0%
where the time goes in v1:
time: 683 us
  waiting for transfers between devices  598 us (88%)
  matrix products  25.9 us (4%)
  local copies, waits for them, and re-layouts  23.6 us (3%)
  between operations  14.2 us (2%)
  other arithmetic  13.6 us (2%)
  starting transfers between devices  7.43 us (1%)
    ppermute x3, waiting for transfers between devices, on_device(): lax.ppermute(ring[-1], 'tm', [(dev, (dev + 1) % 4) for dev in range(4)])  296 us
    all_gather x1, waiting for transfers between devices, on_device(): lax.all_gather(w_qkv, 'tm', axis=1, tiled=True)  190 us
    ppermute x2, waiting for transfers between devices, from_behind(): return lax.ppermute(block, axis, route)  48.2 us
    reduce_scatter x1, waiting for transfers between devices, on_device(): lax.psum_scatter(jnp.concatenate(pieces, axis=0), ('seq', 'mp'), scatter_...  33.1 us
    unnamed x5, waiting for transfers between devices  30.5 us
    unnamed x22, local copies, waits for them, and re-layouts  19.3 us
    dot_general x4, matrix products, on_device(): jnp.einsum('tsh,eh->tse', tokens_part, weight_part, preferred_element_typ...  14.1 us
  transfers between devices with their start and end apart: 9, of which 8 were waited for; matrix products, arithmetic and copies ran while one was open for 3% of the time, Pallas kernels for 0%

profile of v1, /device:TPU:25, one launch (start us, length us, event | category | flops | bytes accessed | tf_op | source)
XLA Modules:
  0.0 682.6 jit_solution(15492071189464584113)
XLA Ops:
  6.5 0.0 copy-start
  6.5 0.0 all-reduce.3.cloned.1.call-start
  7.4 0.1 fusion.24
  7.5 0.6 copy-done
  8.1 1.1 fusion.26
  9.2 0.0 all-reduce.3.cloned.1.call-update
  9.3 0.0 all-gather.3.cloned.1.call-start
  9.3 1.3 convert_reduce_fusion
  10.6 1.4 fusion.10
  12.0 1.3 dynamic-slice.1
  13.3 29.7 %all-reduce.3.cloned.1.call-done = f32[4,15360]{1,0:T(4,128)} async-done(((f32[4,15360]{1,0:T(4,128)}), f32[4,15360]{1,0:T(4,128)}) %all-reduce.3.cloned.1.call-update) | async-done | bytes 245776
  43.0 1.7 dynamic-slice_add_fusion
  44.7 0.0 copy-done.5
  44.7 0.0 copy-start.2
  44.7 0.0 copy-start.6
  44.7 1.1 fusion.13
  45.9 0.0 all-gather.3.cloned.1.call-update
  45.9 0.0 all-gather.5.cloned.1.call-start
  45.9 0.7 all-gather.5.cloned.1.call-update
  46.6 0.0 reduce-scatter.2.cloned.1.call-start
  46.7 0.0 copy-done.2
  46.7 1.4 collective-permute-start
  48.0 40.3 %collective-permute-done = bf16[1280,768]{1,0:T(8,128)(2,1)S(1)} collective-permute-done((bf16[1280,768]{1,0:T(8,128)(2,1)S(1)}, bf16[1280,768]{1,0:T(8,128)(2,1)S(1)}, u32[]{:S(2)}, u32[]{:S(2)}) %collective-permute-start) | collective-permute-done | bytes 1966112 | tf_op jit(solution)/shard_map/ppermute | solution.py:105
  88.3 1.3 copy-done.3
  89.6 3.4 collective-permute-start.1
  93.0 118.6 %collective-permute-done.1 = bf16[1280,768]{1,0:T(8,128)(2,1)} collective-permute-done((bf16[1280,768]{1,0:T(8,128)(2,1)S(1)}, bf16[1280,768]{1,0:T(8,128)(2,1)}, u32[]{:S(2)}, u32[]{:S(2)}) %collective-permute-start.1) | collective-permute-done | bytes 1966112 | tf_op jit(solution)/shard_map/ppermute | solution.py:105
  211.6 0.0 collective-permute-start.2
  211.6 0.0 copy-done.6
  211.6 137.3 %collective-permute-done.2 = bf16[1280,768]{1,0:T(8,128)(2,1)} collective-permute-done((bf16[1280,768]{1,0:T(8,128)(2,1)}, bf16[1280,768]{1,0:T(8,128)(2,1)}, u32[]{:S(2)}, u32[]{:S(2)}) %collective-permute-start.2) | collective-permute-done | bytes 1966112 | tf_op jit(solution)/shard_map/ppermute | solution.py:105
  349.0 3.0 constant_dynamic-update-slice_fusion.7
  352.0 3.0 constant_dynamic-update-slice_fusion.6
  355.0 0.0 copy-done.4
  355.0 1.4 constant_dynamic-update-slice_fusion.5
  356.4 1.4 constant_dynamic-update-slice_fusion.4
  357.8 3.0 constant_dynamic-update-slice_fusion.3
  360.8 2.9 constant_dynamic-update-slice_fusion.2
  363.7 1.4 constant_dynamic-update-slice_fusion.1
  365.1 1.4 constant_dynamic-update-slice_fusion
  366.5 189.9 %all-gather.5.cloned.1.call-done = bf16[3,5120,768]{2,1,0:T(8,128)(2,1)} async-done(((bf16[3,1280,768]{2,1,0:T(8,128)(2,1)}), bf16[3,5120,768]{2,1,0:T(8,128)(2,1)}) %all-gather.5.cloned.1.call-update) | async-done | bytes 23592976 | tf_op jit(solution)/shard_map/all_gather | solution.py:96
  556.4 10.0 %convolution_bitcast_fusion = f32[3,128,768]{2,1,0:T(8,128)S(1)} fusion(bf16[3,5120,768]{2,1,0:T(8,128)(2,1)} %all-gather.5.cloned.1.call-done, bf16[1,128,5120]{2,1,0:T(8,128)(2,1)} %all-gather.3.cloned.1.call-done), kind=kOutput, calls=%fused_computation.13 | convolution fusion | flops 3019898880 | bytes 26083328 | tf_op jit(solution)/shard_map/rd,cdh->crh/dot_general | solution.py:93
  566.4 0.1 slice_multiply_fusion.1
  566.5 0.2 copy.19
  566.7 0.2 copy.21
  566.9 0.2 copy.23
  567.1 0.2 copy.22
  567.3 0.2 copy.20
  567.4 0.5 fusion.15
  568.0 0.2 convolution_convert_fusion
  568.2 3.6 fusion.4
  571.8 3.4 fusion.6
  575.2 3.6 fusion
  578.8 3.4 fusion.2
  582.3 1.7 pad_maximum_fusion
  583.9 0.0 reduce-scatter.2.cloned.1.call-update
  584.0 0.6 dynamic_slice.36
  584.6 1.5 dynamic-slice_reduce_fusion
  586.1 33.1 %reduce-scatter.2.cloned.1.call-done = f32[64,2560]{1,0:T(8,128)} async-done(((f32[256,2560]{1,0:T(8,128)}), f32[64,2560]{1,0:T(8,128)}) %reduce-scatter.2.cloned.1.call-update) | async-done | bytes 655376 | tf_op jit(solution)/shard_map/reduce_scatter | solution.py:123
  619.2 1.7 multiply_multiply_fusion
  620.9 1.3 collective-permute-start.3
  622.2 16.0 %collective-permute-done.3 = f32[64,2560]{1,0:T(8,128)S(1)} collective-permute-done((f32[64,2560]{1,0:T(8,128)S(1)}, f32[64,2560]{1,0:T(8,128)S(1)}, u32[]{:S(2)}, u32[]{:S(2)}) %collective-permute-start.3) | collective-permute-done | bytes 655392 | tf_op jit(solution)/shard_map/ppermute | solution.py:16
  638.2 1.7 fusion.39
  640.0 1.3 collective-permute-start.4
  641.3 32.2 %collective-permute-done.4 = f32[64,2560]{1,0:T(8,128)S(1)} collective-permute-done((f32[64,2560]{1,0:T(8,128)S(1)}, f32[64,2560]{1,0:T(8,128)S(1)}, u32[]{:S(2)}, u32[]{:S(2)}) %collective-permute-start.4) | collective-permute-done | bytes 655392 | tf_op jit(solution)/shard_map/ppermute | solution.py:16
  673.4 2.6 fusion.16
  (16 shorter events, 0.2 us)
Async XLA Ops:
  6.5 1.6 copy-start
  6.5 38.2 %copy-start.5 = (bf16[1,64,5120]{2,1,0:T(8,128)(2,1)S(1)}, bf16[1,64,5120]{2,1,0:T(8,128)(2,1)}, u32[]{:S(2)}) copy-start(bf16[1,64,5120]{2,1,0:T(8,128)(2,1)} %param.6) | copy-start | bytes 1966084
  6.5 36.5 %all-reduce.3.cloned.1.call-start = ((), (), s32[]{:S(2)}) async-start(), calls=%async_computation.4 | async-start | bytes 491520
  9.3 357.3 %all-gather.3.cloned.1.call-start = ((), (), s32[]{:S(2)}) async-start(), calls=%async_computation.1 | async-start | bytes 1966080 | tf_op jit(solution)/shard_map/all_gather | solution.py:88
  44.7 2.0 copy-start.2
  44.7 166.9 %copy-start.6 = (f32[2,768]{1,0:T(2,128)S(1)}, f32[2,768]{1,0:T(2,128)}, u32[]{:S(2)}) copy-start(f32[2,768]{1,0:T(2,128)} %param.9) | copy-start | bytes 18436
  45.9 510.5 %all-gather.5.cloned.1.call-start = ((), (), s32[]{:S(2)}) async-start(), calls=%async_computation.2 | async-start | bytes 29491200 | tf_op jit(solution)/shard_map/all_gather | solution.py:96
  46.6 572.5 %reduce-scatter.2.cloned.1.call-start = ((), (), s32[]{:S(2)}) async-start(), calls=%async_computation.3 | async-start | bytes 3276800 | tf_op jit(solution)/shard_map/reduce_scatter | solution.py:123
  46.7 41.6 %collective-permute-start = (bf16[1280,768]{1,0:T(8,128)(2,1)S(1)}, bf16[1280,768]{1,0:T(8,128)(2,1)S(1)}, u32[]{:S(2)}, u32[]{:S(2)}) collective-permute-start(bf16[1280,768]{1,0:T(8,128)(2,1)S(1)} %copy-done.2), channel_id=1, source_target_pairs={{0,4},{4,8},{8,12},{12,0},{1,5},{5,9},{9,13},{13,1},{2,6},{6,10},{... | collective-permute-start | bytes 5898248 | tf_op jit(solution)/shard_map/ppermute | solution.py:105
  88.3 1.3 copy-start.3
  89.6 122.0 %collective-permute-start.1 = (bf16[1280,768]{1,0:T(8,128)(2,1)S(1)}, bf16[1280,768]{1,0:T(8,128)(2,1)}, u32[]{:S(2)}, u32[]{:S(2)}) collective-permute-start(bf16[1280,768]{1,0:T(8,128)(2,1)S(1)} %collective-permute-done), channel_id=1, source_target_pairs={{0,4},{4,8},{8,12},{12,0},{1,5},{5,9},{9,13},{13,1},{2,6},{6,10},{... | collective-permute-start | bytes 5898248 | tf_op jit(solution)/shard_map/ppermute | solution.py:105
  211.6 137.4 %collective-permute-start.2 = (bf16[1280,768]{1,0:T(8,128)(2,1)}, bf16[1280,768]{1,0:T(8,128)(2,1)}, u32[]{:S(2)}, u32[]{:S(2)}) collective-permute-start(bf16[1280,768]{1,0:T(8,128)(2,1)} %collective-permute-done.1), channel_id=1, source_target_pairs={{0,4},{4,8},{8,12},{12,0},{1,5},{5,9},{9,13},{13,1},{2,6},{6,10},{... | collective-permute-start | bytes 5898248 | tf_op jit(solution)/shard_map/ppermute | solution.py:105
  211.6 143.4 %copy-start.4 = (bf16[1280,768]{1,0:T(8,128)(2,1)S(1)}, bf16[1280,768]{1,0:T(8,128)(2,1)}, u32[]{:S(2)}) copy-start(bf16[1280,768]{1,0:T(8,128)(2,1)} %copy-done.3) | copy-start | bytes 5898244
  583.9 92.1 %copy-start.1 = (bf16[64,15360]{1,0:T(8,128)(2,1)S(1)}, bf16[64,15360]{1,0:T(8,128)(2,1)}, u32[]{:S(2)}) copy-start(bf16[64,15360]{1,0:T(8,128)(2,1)} %param.11) | copy-start | bytes 5898244
  620.9 17.3 %collective-permute-start.3 = (f32[64,2560]{1,0:T(8,128)S(1)}, f32[64,2560]{1,0:T(8,128)S(1)}, u32[]{:S(2)}, u32[]{:S(2)}) collective-permute-start(f32[64,2560]{1,0:T(8,128)S(1)} %multiply_multiply_fusion), channel_id=1, source_target_pairs={{0,4},{4,8},{8,12},{1,5},{5,9},{9,13},{2,6},{6,10},{10,14},{3,7},{... | collective-permute-start | bytes 1966088 | tf_op jit(solution)/shard_map/ppermute | solution.py:16
  640.0 33.5 %collective-permute-start.4 = (f32[64,2560]{1,0:T(8,128)S(1)}, f32[64,2560]{1,0:T(8,128)S(1)}, u32[]{:S(2)}, u32[]{:S(2)}) collective-permute-start(f32[64,2560]{1,0:T(8,128)S(1)} %fusion.39), channel_id=1, source_target_pairs={{0,8},{4,12},{1,9},{5,13},{2,10},{6,14},{3,11},{7,15},{16,24},{20,... | collective-permute-start | bytes 1966088 | tf_op jit(solution)/shard_map/ppermute | solution.py:16
Sparse Core Ops, SparseCore 0:
  9.7 33.3 all-reduce.2
  46.0 27.1 all-gather.2
  74.8 481.5 all-gather.4
  584.1 35.0 reduce-scatter.1
